TPU v7x, 256 devices: a whole 4x4x8 slice. The times are simulated.
256 devices in a mesh: filt: 32 (over y, z_hi, core), space: 8 (over z_lo, x).
Axes of the slice: x: 4, y: 4, z: 8 (z_hi: 4, z_lo: 2; z = z_hi * 2 + z_lo), core: 2. Of those that a mesh axis runs over, the one named last changes fastest.
Arguments:
- volume: bfloat16 [256, 32, 4, 128], P('filt', 'space'), may hold values from -6 to 6
- kernel: bfloat16 [512, 3, 3, 3, 256], P('filt'), may hold values from -0.078125 to 0.078125
- filter_bias: bfloat16 [512], P('filt'), may hold values from -3 to 3
Outputs:
- pooled: bfloat16 [512, 16, 2, 64], P('filt', 'space')
All inputs are finite; a program needn't handle non-finite values.
Results may differ from a plain program's by a relative error of at most 0.001.
Values may be sent and summed in bfloat16 or wider, within the bound.
A program may use at most 64 MiB of HBM per device.

v0:
```python
import jax
import jax.numpy as jnp
from jax import lax
from jax.sharding import PartitionSpec as P

slope = 0.3


def with_halo(block, sides, width):
    for axis, dim in sides:
        count = lax.axis_size(axis)
        forward = [(i, i + 1) for i in range(count - 1)]
        backward = [(target, source) for source, target in forward]
        low = lax.ppermute(
            lax.slice_in_dim(block, block.shape[dim] - width, None, axis=dim), axis, forward
        )
        high = lax.ppermute(lax.slice_in_dim(block, 0, width, axis=dim), axis, backward)
        block = jnp.concatenate([low, block, high], axis=dim)
    return block


def convolve(inputs, weights, padding):
    return lax.conv_general_dilated(
        inputs[None],
        weights,
        (1, 1, 1),
        padding,
        dimension_numbers=("NCDHW", "ODHWI", "NCDHW"),
        preferred_element_type=jnp.float32,
    )[0]


def finish(summed, filter_bias):
    activated = summed + filter_bias.astype(jnp.float32)[:, None, None, None]
    activated = jnp.where(activated > 0, activated, slope * activated)
    filters, depth, height, across = activated.shape
    blocked = activated.reshape(filters, depth // 2, 2, height // 2, 2, across // 2, 2)
    return jnp.max(blocked, axis=(2, 4, 6)).astype(jnp.bfloat16)


def on_device(volume, kernel, filter_bias):
    local_in, slab_depth, height, across = volume.shape
    padded = with_halo(volume, (("space", 1),), 1)
    zeroed = jnp.zeros((kernel.shape[0], slab_depth, height, across), jnp.float32)
    summed = zeroed + convolve(
        lax.all_gather(padded, "filt", axis=0, tiled=True), kernel, ((0, 0), (1, 1), (1, 1))
    )
    return finish(summed, filter_bias)


def solution(mesh):
    in_specs = (P("filt", "space", None, None), P("filt", None, None, None, None), P("filt"))
    out_specs = P("filt", "space", None, None)
    return jax.shard_map(
        on_device, mesh=mesh, in_specs=in_specs, out_specs=out_specs, check_vma=False
    )
```

profile of v0, /device:TPU:1, one launch (start us, length us, event | category | flops | bytes accessed | tf_op | source)
XLA Modules:
  0.0 99.7 jit_solution(1009742245548532842)
XLA Ops:
  6.5 0.0 copy-start
  6.5 0.0 all-gather.2.cloned.1.call-start
  6.5 0.8 fusion.16
  7.3 3.9 %collective-permute-start = (bf16[8,1,4,128]{3,2,1,0:T(4,128)(2,1)S(1)}, bf16[8,1,4,128]{3,2,1,0:T(4,128)(2,1)S(1)}, u32[]{:S(2)}, u32[]{:S(2)}) collective-permute-start(bf16[8,1,4,128]{3,2,1,0:T(4,128)(2,1)S(1)} %get-tuple-element.5), channel_id=1, source_target_pairs={{0,1},{1,2},{2,3},{3,4},{4,5},{5,6},{6,7},{8,9},{9,10},{10,11},{11... | collective-permute-start | bytes 24584 | tf_op jit(solution)/shard_map/ppermute | solution.py:14
  11.2 1.3 %collective-permute-start.1 = (bf16[8,1,4,128]{3,2,1,0:T(4,128)(2,1)S(1)}, bf16[8,1,4,128]{3,2,1,0:T(4,128)(2,1)S(1)}, u32[]{:S(2)}, u32[]{:S(2)}) collective-permute-start(bf16[8,1,4,128]{3,2,1,0:T(4,128)(2,1)S(1)} %get-tuple-element.6), channel_id=1, source_target_pairs={{1,0},{2,1},{3,2},{4,3},{5,4},{6,5},{7,6},{9,8},{10,9},{11,10},{12... | collective-permute-start | bytes 24584 | tf_op jit(solution)/shard_map/ppermute | solution.py:17
  12.5 0.0 collective-permute-done
  12.6 3.1 %collective-permute-done.1 = bf16[8,1,4,128]{3,2,1,0:T(4,128)(2,1)S(1)} collective-permute-done((bf16[8,1,4,128]{3,2,1,0:T(4,128)(2,1)S(1)}, bf16[8,1,4,128]{3,2,1,0:T(4,128)(2,1)S(1)}, u32[]{:S(2)}, u32[]{:S(2)}) %collective-permute-start.1) | collective-permute-done | bytes 8224 | tf_op jit(solution)/shard_map/ppermute | solution.py:17
  15.6 1.4 %pad_maximum_fusion = bf16[8,6,4,128]{3,2,1,0:T(4,128)(2,1)} fusion(bf16[8,1,4,128]{3,2,1,0:T(4,128)(2,1)S(1)} %collective-permute-done.1, bf16[8,4,4,128]{3,2,1,0:T(4,128)(2,1)} %param.3, bf16[8,1,4,128]{3,2,1,0:T(4,128)(2,1)S(1)} %collective-permute-done), kind=kLoop, calls=%fused_computation.13 | loop fusion | flops 49152 | bytes 98304 | tf_op jit(solution)/shard_map/concatenate | solution.py:18
  17.1 0.0 all-gather.2.cloned.1.call-update
  17.1 0.7 convert_element_type.6
  17.7 58.8 %all-gather.2.cloned.1.call-done = bf16[256,6,4,128]{3,2,1,0:T(4,128)(2,1)} async-done(((bf16[8,6,4,128]{3,2,1,0:T(4,128)(2,1)}), bf16[256,6,4,128]{3,2,1,0:T(4,128)(2,1)}) %all-gather.2.cloned.1.call-update) | async-done | bytes 1572880 | tf_op jit(solution)/shard_map/all_gather | solution.py:46
  76.5 3.2 %copy.26 = bf16[256,6,4,1,128]{0,2,4,1,3:T(4,128)(2,1)S(1)} copy(bf16[256,6,4,1,128]{4,2,1,0,3:T(4,128)(2,1)} %bitcast.17) | data formatting | bytes 3145728
  79.8 0.6 pad.clone
  80.4 0.0 copy-start.1
  80.4 0.2 copy.21
  80.7 0.0 copy-done
  80.7 0.4 copy-done.1
  81.1 8.4 %fusion.8 = f32[4,4,8,17,16]{4,2,3,1,0:T(8,128)S(1)} fusion(bf16[16,3,3,3,256]{4,0,3,2,1:T(8,128)(2,1)S(1)} %copy-done, bf16[256,6,4,1,7,2]{0,4,5,2,1,3:T(8,128)(2,1)S(1)} %slice.10, bf16[256,6,4,1,8,17]{0,4,5,2,1,3:T(8,128)(2,1)S(1)} %copy.21, pred[8,17]{0,1:T(8,128)(4,1)S(1)} %copy-done.1), kind=kOutput, calls=%fused_computation.9 | convolution fusion | flops 406718464 | bytes 2203784 | tf_op jit(solution)/shard_map/conv_general_dilated | solution.py:23
  89.5 0.8 copy.22
  90.3 0.3 reshape.9
  90.7 0.3 copy.23
  91.0 1.2 %fusion.11 = bf16[16,2,2,64]{0,3,2,1:T(8,128)(2,1)S(1)} fusion(f32[16,2,2,2,2,64,2]{0,6,5,4,3,2,1:T(2,128)S(1)} %bitcast.16, f32[16]{0:T(128)S(1)} %convert_element_type.6), kind=kLoop, calls=%fused_computation.10 | loop fusion | flops 159744 | bytes 139328 | tf_op jit(solution)/shard_map/reduce_max | solution.py:38
  92.2 0.1 copy.24
  92.3 0.6 copy.25
  (2 shorter events, 0.1 us)
Async XLA Ops:
  6.5 74.2 %copy-start = (bf16[16,3,3,3,256]{4,0,3,2,1:T(8,128)(2,1)S(1)}, bf16[16,3,3,3,256]{4,0,3,2,1:T(8,128)(2,1)}, u32[]{:S(2)}) copy-start(bf16[16,3,3,3,256]{4,0,3,2,1:T(8,128)(2,1)} %param.4) | copy-start | bytes 663556
  6.5 70.0 %all-gather.2.cloned.1.call-start = ((), (), s32[]{:S(2)}) async-start(), calls=%async_computation | async-start | bytes 1622016 | tf_op jit(solution)/shard_map/all_gather | solution.py:46
  7.3 5.2 %collective-permute-start = (bf16[8,1,4,128]{3,2,1,0:T(4,128)(2,1)S(1)}, bf16[8,1,4,128]{3,2,1,0:T(4,128)(2,1)S(1)}, u32[]{:S(2)}, u32[]{:S(2)}) collective-permute-start(bf16[8,1,4,128]{3,2,1,0:T(4,128)(2,1)S(1)} %get-tuple-element.5), channel_id=1, source_target_pairs={{0,1},{1,2},{2,3},{3,4},{4,5},{5,6},{6,7},{8,9},{9,10},{10,11},{11... | collective-permute-start | bytes 24584 | tf_op jit(solution)/shard_map/ppermute | solution.py:14
  11.2 4.4 %collective-permute-start.1 = (bf16[8,1,4,128]{3,2,1,0:T(4,128)(2,1)S(1)}, bf16[8,1,4,128]{3,2,1,0:T(4,128)(2,1)S(1)}, u32[]{:S(2)}, u32[]{:S(2)}) collective-permute-start(bf16[8,1,4,128]{3,2,1,0:T(4,128)(2,1)S(1)} %get-tuple-element.6), channel_id=1, source_target_pairs={{1,0},{2,1},{3,2},{4,3},{5,4},{6,5},{7,6},{9,8},{10,9},{11,10},{12... | collective-permute-start | bytes 24584 | tf_op jit(solution)/shard_map/ppermute | solution.py:17
  80.4 0.7 copy-start.1
Sparse Core Ops, SparseCore 0:
  17.2 59.2 all-gather.1
where the time goes:
time: 100 us; the launch traced here: 99.7 us
  waiting for transfers between devices  61.9 us (62%)
  between operations  13.5 us (14%)
  matrix products  8.37 us (8%)
  local copies, waits for them, and re-layouts  7.48 us (7%)
  starting transfers between devices  5.23 us (5%)
  other arithmetic  3.25 us (3%)
    all_gather x1, waiting for transfers between devices, on_device(): lax.all_gather(padded, 'filt', axis=0, tiled=True)  58.8 us
    conv_general_dilated x1, matrix products, convolve(): lax.conv_general_dilated(inputs[None], weights, (1, 1, 1), padding, dimen...  8.37 us
    ppermute x1, starting transfers between devices, with_halo(): lax.ppermute(lax.slice_in_dim(block, block.shape[dim] - width, None, axis...  3.94 us
    unnamed x5, local copies, waits for them, and re-layouts  3.63 us
    ppermute x1, waiting for transfers between devices, with_halo(): lax.ppermute(lax.slice_in_dim(block, 0, width, axis=dim), axis, backward)  3.08 us
  transfers between devices with their start and end apart: 3, of which 2 were waited for; matrix products, arithmetic and copies ran while one was open for 1% of the time, Pallas kernels for 0%

commit v1 on v0

--- a/solution.py
+++ b/solution.py
@@ -4,6 +4,13 @@
 from jax.sharding import PartitionSpec as P
 
 slope = 0.3
+
+
+def _supply_all_rings(message):
+    f_next = lax.axis_size("filt")
+    oldest = jnp.stack([message] * f_next, 0)
+    state_next = lax.all_to_all(oldest, concat_axis=0, axis_name="filt", split_axis=0)
+    return jnp.concatenate(state_next, axis=0)
 
 
 def with_halo(block, sides, width):
@@ -42,9 +49,7 @@
     local_in, slab_depth, height, across = volume.shape
     padded = with_halo(volume, (("space", 1),), 1)
     zeroed = jnp.zeros((kernel.shape[0], slab_depth, height, across), jnp.float32)
-    summed = zeroed + convolve(
-        lax.all_gather(padded, "filt", axis=0, tiled=True), kernel, ((0, 0), (1, 1), (1, 1))
-    )
+    summed = zeroed + convolve(_supply_all_rings(padded), kernel, ((0, 0), (1, 1), (1, 1)))
     return finish(summed, filter_bias)
 
 

time: 100 us -> 80 us (0.80)
  the two profiles are of different devices: /device:TPU:1 before, /device:TPU:2 now
where the time goes in v1:
time: 80 us; the launch traced here: 79.7 us
  waiting for transfers between devices  44.5 us (56%)
  starting transfers between devices  17.4 us (22%)
  matrix products  8.38 us (10%)
  local copies, waits for them, and re-layouts  7.26 us (9%)
  other arithmetic  1.98 us (2%)
    all_to_all x1, waiting for transfers between devices, _supply_all_rings(): lax.all_to_all(oldest, concat_axis=0, axis_name='filt', split_axis=0)  41.4 us
    all_to_all x1, starting transfers between devices, _supply_all_rings(): lax.all_to_all(oldest, concat_axis=0, axis_name='filt', split_axis=0)  11.6 us
    conv_general_dilated x1, matrix products, convolve(): lax.conv_general_dilated(inputs[None], weights, (1, 1, 1), padding, dimen...  8.38 us
    ppermute x1, starting transfers between devices, with_halo(): lax.ppermute(lax.slice_in_dim(block, block.shape[dim] - width, None, axis...  3.39 us
    ppermute x1, waiting for transfers between devices, with_halo(): lax.ppermute(lax.slice_in_dim(block, 0, width, axis=dim), axis, backward)  3.09 us
    ppermute x1, starting transfers between devices, with_halo(): lax.ppermute(lax.slice_in_dim(block, 0, width, axis=dim), axis, backward)  2.44 us
    conv_general_dilated x6, local copies, waits for them, and re-layouts, convolve(): lax.conv_general_dilated(inputs[None], weights, (1, 1, 1), padding, dimen...  1.75 us
  transfers between devices with their start and end apart: 3, of which 2 were waited for; matrix products, arithmetic and copies ran while one was open for 0% of the time, Pallas kernels for 0%

profile of v1, /device:TPU:2, one launch (start us, length us, event | category | flops | bytes accessed | tf_op | source)
XLA Modules:
  0.0 79.7 jit_solution(10329640561818853407)
XLA Ops:
  0.0 0.0 copy-start
  0.0 0.8 fusion.16
  0.8 3.4 %collective-permute-start = (bf16[8,1,4,128]{3,2,1,0:T(4,128)(2,1)S(1)}, bf16[8,1,4,128]{3,2,1,0:T(4,128)(2,1)S(1)}, u32[]{:S(2)}, u32[]{:S(2)}) collective-permute-start(bf16[8,1,4,128]{3,2,1,0:T(4,128)(2,1)S(1)} %get-tuple-element.5), channel_id=1, source_target_pairs={{0,1},{1,2},{2,3},{3,4},{4,5},{5,6},{6,7},{8,9},{9,10},{10,11},{11... | collective-permute-start | bytes 24584 | tf_op jit(solution)/shard_map/ppermute | solution.py:21
  4.2 2.4 %collective-permute-start.1 = (bf16[8,1,4,128]{3,2,1,0:T(4,128)(2,1)S(1)}, bf16[8,1,4,128]{3,2,1,0:T(4,128)(2,1)S(1)}, u32[]{:S(2)}, u32[]{:S(2)}) collective-permute-start(bf16[8,1,4,128]{3,2,1,0:T(4,128)(2,1)S(1)} %get-tuple-element.6), channel_id=1, source_target_pairs={{1,0},{2,1},{3,2},{4,3},{5,4},{6,5},{7,6},{9,8},{10,9},{11,10},{12... | collective-permute-start | bytes 24584 | tf_op jit(solution)/shard_map/ppermute | solution.py:24
  6.6 0.0 collective-permute-done
  6.6 3.1 %collective-permute-done.1 = bf16[8,1,4,128]{3,2,1,0:T(4,128)(2,1)S(1)} collective-permute-done((bf16[8,1,4,128]{3,2,1,0:T(4,128)(2,1)S(1)}, bf16[8,1,4,128]{3,2,1,0:T(4,128)(2,1)S(1)}, u32[]{:S(2)}, u32[]{:S(2)}) %collective-permute-start.1) | collective-permute-done | bytes 8224 | tf_op jit(solution)/shard_map/ppermute | solution.py:24
  9.7 0.8 %pad_maximum_fusion = bf16[8,6,4,128]{3,2,1,0:T(4,128)(2,1)S(1)} fusion(bf16[8,1,4,128]{3,2,1,0:T(4,128)(2,1)S(1)} %collective-permute-done.1, bf16[8,4,4,128]{3,2,1,0:T(4,128)(2,1)} %param.3, bf16[8,1,4,128]{3,2,1,0:T(4,128)(2,1)S(1)} %collective-permute-done), kind=kLoop, calls=%fused_computation.14 | loop fusion | flops 49152 | bytes 98304 | tf_op jit(solution)/shard_map/concatenate | solution.py:25
  10.5 1.5 %stack.2 = bf16[32,8,6,4,128]{4,1,3,2,0:T(8,128)(2,1)} broadcast(bf16[8,6,4,128]{3,0,2,1:T(8,128)(2,1)S(1)} %copy.22), dimensions={1,2,3,4} | broadcast | bytes 1622016 | tf_op jit(solution)/shard_map/stack | solution.py:11
  12.0 11.6 %all-to-all-start = ((bf16[32,8,6,4,128]{4,1,3,2,0:T(8,128)(2,1)}), bf16[32,8,6,4,128]{4,1,3,2,0:T(8,128)(2,1)S(1)}, u32[]{:S(2)}, u32[]{:S(2)}) async-start(bf16[32,8,6,4,128]{4,1,3,2,0:T(8,128)(2,1)} %stack.2), calls=%async_computation | async-start | bytes 3145728 | tf_op jit(solution)/shard_map/all_to_all | solution.py:12
  23.7 0.0 copy-done.1
  23.7 41.4 %all-to-all-done = bf16[32,8,6,4,128]{4,1,3,2,0:T(8,128)(2,1)S(1)} async-done(((bf16[32,8,6,4,128]{4,1,3,2,0:T(8,128)(2,1)}), bf16[32,8,6,4,128]{4,1,3,2,0:T(8,128)(2,1)S(1)}, u32[]{:S(2)}, u32[]{:S(2)}) %all-to-all-start) | async-done | bytes 1572896 | tf_op jit(solution)/shard_map/all_to_all | solution.py:12
  65.1 0.4 copy.33
  65.5 1.1 %copy.31 = bf16[256,6,4,1,128]{0,2,4,1,3:T(4,128)(2,1)S(1)} copy(bf16[256,6,4,1,128]{4,0,2,1,3:T(8,128)(2,1)S(1)} %bitcast.18) | data formatting | bytes 3145728
  66.6 0.6 pad.clone
  67.2 0.0 copy-start.2
  67.2 0.2 copy.26
  67.5 0.4 copy-done.2
  67.9 8.4 %fusion.8 = f32[4,4,8,17,16]{4,2,3,1,0:T(8,128)S(1)} fusion(bf16[16,3,3,3,256]{4,0,3,2,1:T(8,128)(2,1)S(1)} %copy-done, bf16[256,6,4,1,7,2]{0,4,5,2,1,3:T(8,128)(2,1)S(1)} %slice.10, bf16[256,6,4,1,8,17]{0,4,5,2,1,3:T(8,128)(2,1)S(1)} %copy.26, pred[8,17]{0,1:T(8,128)(4,1)S(1)} %copy-done.2), kind=kOutput, calls=%fused_computation.10 | convolution fusion | flops 406718464 | bytes 2203784 | tf_op jit(solution)/shard_map/conv_general_dilated | solution.py:30
  76.3 0.8 %copy.27 = f32[4,4,8,17,16]{3,2,4,1,0:T(8,128)S(1)} copy(f32[4,4,8,17,16]{4,2,3,1,0:T(8,128)S(1)} %fusion.8) | data formatting | bytes 278528 | tf_op jit(solution)/shard_map/conv_general_dilated | solution.py:30
  77.1 0.3 reshape.11
  77.5 0.3 copy.28
  77.8 1.2 %fusion.11 = bf16[16,2,2,64]{0,3,2,1:T(8,128)(2,1)S(1)} fusion(f32[16,2,2,2,2,64,2]{0,6,5,4,3,2,1:T(2,128)S(1)} %bitcast.19, f32[16]{0:T(128)S(1)} %convert_element_type.6), kind=kLoop, calls=%fused_computation.11 | loop fusion | flops 159744 | bytes 139328 | tf_op jit(solution)/shard_map/reduce_max | solution.py:45
  79.0 0.1 copy.29
  79.1 0.6 copy.30
  (6 shorter events, 0.1 us)
Async XLA Ops:
  0.0 67.5 %copy-start = (bf16[16,3,3,3,256]{4,0,3,2,1:T(8,128)(2,1)S(1)}, bf16[16,3,3,3,256]{4,0,3,2,1:T(8,128)(2,1)}, u32[]{:S(2)}) copy-start(bf16[16,3,3,3,256]{4,0,3,2,1:T(8,128)(2,1)} %param.4) | copy-start | bytes 663556
  0.8 5.8 %collective-permute-start = (bf16[8,1,4,128]{3,2,1,0:T(4,128)(2,1)S(1)}, bf16[8,1,4,128]{3,2,1,0:T(4,128)(2,1)S(1)}, u32[]{:S(2)}, u32[]{:S(2)}) collective-permute-start(bf16[8,1,4,128]{3,2,1,0:T(4,128)(2,1)S(1)} %get-tuple-element.5), channel_id=1, source_target_pairs={{0,1},{1,2},{2,3},{3,4},{4,5},{5,6},{6,7},{8,9},{9,10},{10,11},{11... | collective-permute-start | bytes 24584 | tf_op jit(solution)/shard_map/ppermute | solution.py:21
  4.2 5.5 %collective-permute-start.1 = (bf16[8,1,4,128]{3,2,1,0:T(4,128)(2,1)S(1)}, bf16[8,1,4,128]{3,2,1,0:T(4,128)(2,1)S(1)}, u32[]{:S(2)}, u32[]{:S(2)}) collective-permute-start(bf16[8,1,4,128]{3,2,1,0:T(4,128)(2,1)S(1)} %get-tuple-element.6), channel_id=1, source_target_pairs={{1,0},{2,1},{3,2},{4,3},{5,4},{6,5},{7,6},{9,8},{10,9},{11,10},{12... | collective-permute-start | bytes 24584 | tf_op jit(solution)/shard_map/ppermute | solution.py:24
  12.0 11.6 %copy-start.1 = (bf16[16]{0:T(256)(128)(2,1)S(1)}, bf16[16]{0:T(256)(128)(2,1)}, u32[]{:S(2)}) copy-start(bf16[16]{0:T(256)(128)(2,1)} %param.5) | copy-start | bytes 100
  12.0 53.0 %all-to-all-start = ((bf16[32,8,6,4,128]{4,1,3,2,0:T(8,128)(2,1)}), bf16[32,8,6,4,128]{4,1,3,2,0:T(8,128)(2,1)S(1)}, u32[]{:S(2)}, u32[]{:S(2)}) async-start(bf16[32,8,6,4,128]{4,1,3,2,0:T(8,128)(2,1)} %stack.2), calls=%async_computation | async-start | bytes 3145728 | tf_op jit(solution)/shard_map/all_to_all | solution.py:12
  67.2 0.7 copy-start.2
